TPU v7x, 1024 devices: a whole 8x8x8 slice. The times are simulated.
1024 devices in a mesh: gx: 4 (over x_hi, core), gy: 4 (over x_lo), gz: 64 (over z, y).
Axes of the slice: x: 8 (x_hi: 2, x_lo: 4; x = x_hi * 4 + x_lo), y: 8, z: 8, core: 2. Of those that a mesh axis runs over, the one named last changes fastest.
Arguments:
- positions: float32 [3, 4, 4, 128, 256], P(None, 'gx', 'gy', 'gz'), may hold values from 0 to 1
- velocities: float32 [3, 4, 4, 128, 256], P(None, 'gx', 'gy', 'gz'), may hold values from -2 to 2
- mass: float32 [4, 4, 128, 256], P('gx', 'gy', 'gz'), may hold values from 0.03 to 0.3
- counts: int32 [4, 4, 128], P('gx', 'gy', 'gz'), may hold values from 1 to 256, as said below
Outputs:
- new_positions: float32 [3, 4, 4, 128, 256], P(None, 'gx', 'gy', 'gz')
- new_velocities: float32 [3, 4, 4, 128, 256], P(None, 'gx', 'gy', 'gz')
Inputs may be any that keep to these rules, and one draw needn't show every extreme that they name: `counts`: particles of a bin fill its first slots; every bin holds at least 128 particles, and some bin holds exactly 256 particles in every draw.
All inputs are finite; a program needn't handle non-finite values.
Results may differ from a plain program's by a relative error of at most 0.0001.
Values sent between devices are 32-bit elements; how exact they have to be, the bound alone decides.
A program may use at most 32 MiB of HBM per device.

v0:
```python
import jax
import jax.numpy as jnp
from jax import lax
from jax.sharding import PartitionSpec as P

SUBCYCLES = 2


time_step = 0.25


def with_halo(array, sides, width):
    for axis, dim in sides:
        size, length = (lax.axis_size(axis), array.shape[dim])
        up = [(i, (i + 1) % size) for i in range(size)]
        down = [(j, i) for i, j in up]
        last = lax.slice_in_dim(array, length - width, length, axis=dim)
        initial = lax.slice_in_dim(array, 0, width, axis=dim)
        before = lax.ppermute(last, axis, up)
        after = lax.ppermute(initial, axis, down)
        array = jnp.concatenate([before, array, after], axis=dim)
    return array


def accelerations(target, shell_place, shell_mass):
    slots = target.shape[-1]
    size_x, size_y, size_z = (target.shape[1], target.shape[2], target.shape[3])
    bin_count = size_x * size_y * size_z
    target_flat = target.reshape(3, bin_count, slots)
    total = jnp.zeros((3, bin_count, slots), jnp.float32)
    for shift_x in range(3):
        for shift_y in range(3):
            for shift_z in range(3):
                source = shell_place[
                    :,
                    shift_x : shift_x + size_x,
                    shift_y : shift_y + size_y,
                    shift_z : shift_z + size_z,
                    :,
                ]
                source = source.reshape(3, bin_count, slots)
                source_mass = shell_mass[
                    shift_x : shift_x + size_x,
                    shift_y : shift_y + size_y,
                    shift_z : shift_z + size_z,
                    :,
                ]
                source_mass = source_mass.reshape(bin_count, slots)
                offset = jnp.array([shift_x - 1.0, shift_y - 1.0, shift_z - 1.0], jnp.float32)
                delta = (
                    offset[:, None, None, None] + source[:, :, None, :] - target_flat[:, :, :, None]
                )
                squared = jnp.sum(delta * delta, axis=0)
                falloff = jnp.maximum(1.0 - squared, 0.0)
                weighted = falloff * falloff * falloff * source_mass[:, None, :]
                total = total + jnp.sum(delta * weighted[None], axis=-1)
    return total.reshape(target.shape)


def shell_packed(packed):
    taller = with_halo(packed, (("gz", 3),), 1)
    return with_halo(taller, (("gx", 1), ("gy", 2)), 1)


def shell_plain(place):
    taller = with_halo(place, (("gz", 3),), 1)
    return with_halo(taller, (("gx", 1), ("gy", 2)), 1)


def on_device(positions, velocities, mass, counts):
    occupied = lax.broadcasted_iota(jnp.int32, mass.shape, 3) < counts[..., None]
    weight = jnp.where(occupied, mass, jnp.zeros_like(mass))
    place = positions
    speed = velocities
    shell_mass = weight
    for subcycle in range(SUBCYCLES):
        if subcycle == 0:
            packed = jnp.concatenate([place, weight[None]], axis=0)
            shell_data = shell_packed(packed)
            shell_place = shell_data[:3]
            shell_mass = shell_data[3]
        else:
            shell_place = shell_plain(place)
        accel = accelerations(place, shell_place, shell_mass)
        speed = speed + time_step * accel
        place = jnp.clip(place + time_step * speed, 0.0, 1.0)
    new_positions = jnp.where(occupied[None], place, jnp.zeros_like(place))
    new_velocities = jnp.where(occupied[None], speed, jnp.zeros_like(speed))
    return (new_positions, new_velocities)


def solution(mesh):
    placed = (
        P(None, "gx", "gy", "gz", None),
        P(None, "gx", "gy", "gz", None),
        P("gx", "gy", "gz", None),
        P("gx", "gy", "gz"),
    )
    return jax.shard_map(
        on_device,
        mesh=mesh,
        in_specs=placed,
        out_specs=(P(None, "gx", "gy", "gz", None), P(None, "gx", "gy", "gz", None)),
        check_vma=False,
    )
```

profile of v0, /device:TPU:1, one launch (start us, length us, event | category | flops | bytes accessed | tf_op | source)
XLA Modules:
  0.0 120.5 jit_solution(7588956539299302740)
XLA Ops:
  0.6 0.8 fusion.231
  1.4 0.8 fusion.230
  2.2 4.1 %collective-permute-start = (f32[4,1,1,1,256]{4,3,0,2,1:T(1,128)S(1)}, f32[4,1,1,1,256]{4,3,0,2,1:T(1,128)S(1)}, u32[]{:S(2)}, u32[]{:S(2)}) collective-permute-start(f32[4,1,1,1,256]{4,3,0,2,1:T(1,128)S(1)} %get-tuple-element.187), channel_id=1, source_target_pairs={{0,1},{1,2},{2,3},{3,4},{4,5},{5,6},{6,7},{7,8},{8,9},{9,10},{10,1... | collective-permute-start | bytes 12296 | tf_op jit(solution)/shard_map/ppermute | solution.py:19
  6.3 19.3 %collective-permute-start.1 = (f32[4,1,1,1,256]{4,3,0,2,1:T(1,128)S(1)}, f32[4,1,1,1,256]{4,3,0,2,1:T(1,128)S(1)}, u32[]{:S(2)}, u32[]{:S(2)}) collective-permute-start(f32[4,1,1,1,256]{4,3,0,2,1:T(1,128)S(1)} %get-tuple-element.188), channel_id=1, source_target_pairs={{1,0},{2,1},{3,2},{4,3},{5,4},{6,5},{7,6},{8,7},{9,8},{10,9},{11,1... | collective-permute-start | bytes 12296 | tf_op jit(solution)/shard_map/ppermute | solution.py:20
  25.7 0.7 collective-permute-done.1
  26.4 0.7 pad_maximum_fusion.2
  27.1 8.5 %collective-permute-start.2 = (f32[4,1,1,4,256]{4,3,0,2,1:T(4,128)S(1)}, f32[4,1,1,4,256]{4,3,0,2,1:T(4,128)S(1)}, u32[]{:S(2)}, u32[]{:S(2)}) collective-permute-start(f32[4,1,1,4,256]{4,3,0,2,1:T(4,128)S(1)} %pad_maximum_fusion.2), channel_id=1, source_target_pairs={{0,256},{256,512},{512,768},{768,0},{1,257},{257,513},{513,769},{7... | collective-permute-start | bytes 49160 | tf_op jit(solution)/shard_map/ppermute | solution.py:19
  35.7 1.9 %collective-permute-start.3 = (f32[4,1,1,4,256]{4,3,0,2,1:T(4,128)S(1)}, f32[4,1,1,4,256]{4,3,0,2,1:T(4,128)S(1)}, u32[]{:S(2)}, u32[]{:S(2)}) collective-permute-start(f32[4,1,1,4,256]{4,3,0,2,1:T(4,128)S(1)} %pad_maximum_fusion.2), channel_id=1, source_target_pairs={{256,0},{512,256},{768,512},{0,768},{257,1},{513,257},{769,513},{1... | collective-permute-start | bytes 49160 | tf_op jit(solution)/shard_map/ppermute | solution.py:20
  37.6 0.8 fusion.211
  38.4 6.4 %collective-permute-done.3 = f32[4,1,1,4,256]{4,3,0,2,1:T(4,128)S(1)} collective-permute-done((f32[4,1,1,4,256]{4,3,0,2,1:T(4,128)S(1)}, f32[4,1,1,4,256]{4,3,0,2,1:T(4,128)S(1)}, u32[]{:S(2)}, u32[]{:S(2)}) %collective-permute-start.3) | collective-permute-done | bytes 16416 | tf_op jit(solution)/shard_map/ppermute | solution.py:20
  44.8 0.7 pad_maximum_fusion
  45.5 2.2 %collective-permute-start.4 = (f32[4,3,1,4,256]{4,3,0,2,1:T(4,128)S(1)}, f32[4,3,1,4,256]{4,3,0,2,1:T(4,128)S(1)}, u32[]{:S(2)}, u32[]{:S(2)}) collective-permute-start(f32[4,3,1,4,256]{4,3,0,2,1:T(4,128)S(1)} %pad_maximum_fusion), channel_id=1, source_target_pairs={{0,64},{64,128},{128,192},{192,0},{1,65},{65,129},{129,193},{193,1... | collective-permute-start | bytes 147464 | tf_op jit(solution)/shard_map/ppermute | solution.py:19
  47.7 4.9 %collective-permute-start.5 = (f32[4,3,1,4,256]{4,3,0,2,1:T(4,128)S(1)}, f32[4,3,1,4,256]{4,3,0,2,1:T(4,128)S(1)}, u32[]{:S(2)}, u32[]{:S(2)}) collective-permute-start(f32[4,3,1,4,256]{4,3,0,2,1:T(4,128)S(1)} %pad_maximum_fusion), channel_id=1, source_target_pairs={{64,0},{128,64},{192,128},{0,192},{65,1},{129,65},{193,129},{1,193... | collective-permute-start | bytes 147464 | tf_op jit(solution)/shard_map/ppermute | solution.py:20
  52.6 0.8 fusion.201
  53.4 0.8 fusion.220
  55.6 2.4 %fusion.2 = (f32[2,256,256]{2,1,0:T(8,128)S(1)}, f32[2,256,256]{2,1,0:T(8,128)S(1)}, f32[2,256,256]{2,1,0:T(8,128)S(1)}, f32[2,256,256]{2,1,0:T(8,128)S(1)}, f32...) fusion(f32[3,2,256]{2,1,0:T(2,128)S(1)} %get-tuple-element.121,, ...), kind=kLoop, calls=%fused_computation.110 | loop fusion | flops 10615296 | bytes 5316608 | tf_op jit(solution)/shard_map/reduce_sum | solution.py:53
  58.1 4.5 %fusion.3 = (f32[3,2,256]{2,1,0:T(2,128)S(1)}, f32[2,256,256]{2,1,0:T(8,128)S(1)}, f32[2,256,256]{2,1,0:T(8,128)S(1)}, f32[2,256,256]{2,1,0:T(8,128)S(1)}, f32[2...) fusion(f32[2,256,256]{2,1,0:T(8,128)S(1)} %fusion.109, ...), kind=kLoop, calls=%fused_computation.111 | loop fusion | flops 19003904 | bytes 9553920 | tf_op jit(solution)/shard_map/reduce_sum | solution.py:56
  64.9 2.0 %fusion.9 = (f32[3,2,256]{2,1,0:T(2,128)S(1)}, f32[3,2,256]{2,1,0:T(2,128)S(1)}, f32[3,2,256]{2,1,0:T(2,128)S(1)}, f32[3,2,256]{2,1,0:T(2,128)S(1)}, f32[3,2,256...) fusion(f32[2,256,256]{2,1,0:T(8,128)S(1)} %get-tuple-element.195, ...), kind=kLoop, calls=%fused_computation.117 | loop fusion | flops 8246784 | bytes 3756032 | tf_op jit(solution)/shard_map/reduce_sum | solution.py:56
  66.9 2.4 %fusion.7 = (f32[3,2,256]{2,1,0:T(2,128)S(1)}, f32[3,2,256]{2,1,0:T(2,128)S(1)}, f32[3,2,256]{2,1,0:T(2,128)S(1)}, f32[3,2,256]{2,1,0:T(2,128)S(1)}, f32[3,2,256...) fusion(f32[2,256,256]{2,1,0:T(8,128)S(1)} %get-tuple-element.19, ...), kind=kLoop, calls=%fused_computation.115 | loop fusion | flops 10603008 | bytes 4835328 | tf_op jit(solution)/shard_map/reduce_sum | solution.py:56
  69.4 2.4 %fusion.5 = (f32[3,2,256]{2,1,0:T(2,128)S(1)}, f32[3,2,256]{2,1,0:T(2,128)S(1)}, f32[3,2,256]{2,1,0:T(2,128)S(1)}, f32[3,2,256]{2,1,0:T(2,128)S(1)}, f32[3,2,256...) fusion(f32[2,256,256]{2,1,0:T(8,128)S(1)} %get-tuple-element.19, ...), kind=kLoop, calls=%fused_computation.113 | loop fusion | flops 10603008 | bytes 4835328 | tf_op jit(solution)/shard_map/reduce_sum | solution.py:56
  71.9 1.9 %collective-permute-start.6 = (f32[3,1,1,1,256]{4,3,0,2,1:T(1,128)S(1)}, f32[3,1,1,1,256]{4,3,0,2,1:T(1,128)S(1)}, u32[]{:S(2)}, u32[]{:S(2)}) collective-permute-start(f32[3,1,1,1,256]{4,3,0,2,1:T(1,128)S(1)} %get-tuple-element.191), channel_id=1, source_target_pairs={{0,1},{1,2},{2,3},{3,4},{4,5},{5,6},{6,7},{7,8},{8,9},{9,10},{10,1... | collective-permute-start | bytes 9224 | tf_op jit(solution)/shard_map/ppermute | solution.py:19
  73.8 7.2 %collective-permute-start.7 = (f32[3,1,1,1,256]{4,3,0,2,1:T(1,128)S(1)}, f32[3,1,1,1,256]{4,3,0,2,1:T(1,128)S(1)}, u32[]{:S(2)}, u32[]{:S(2)}) collective-permute-start(f32[3,1,1,1,256]{4,3,0,2,1:T(1,128)S(1)} %get-tuple-element.192), channel_id=1, source_target_pairs={{1,0},{2,1},{3,2},{4,3},{5,4},{6,5},{7,6},{8,7},{9,8},{10,9},{11,1... | collective-permute-start | bytes 9224 | tf_op jit(solution)/shard_map/ppermute | solution.py:20
  81.8 3.3 %collective-permute-start.8 = (f32[3,1,1,4,256]{4,3,0,2,1:T(4,128)S(1)}, f32[3,1,1,4,256]{4,3,0,2,1:T(4,128)S(1)}, u32[]{:S(2)}, u32[]{:S(2)}) collective-permute-start(f32[3,1,1,4,256]{4,3,0,2,1:T(4,128)S(1)} %pad_maximum_fusion.3), channel_id=1, source_target_pairs={{0,256},{256,512},{512,768},{768,0},{1,257},{257,513},{513,769},{7... | collective-permute-start | bytes 36872 | tf_op jit(solution)/shard_map/ppermute | solution.py:19
  85.2 1.9 %collective-permute-start.9 = (f32[3,1,1,4,256]{4,3,0,2,1:T(4,128)S(1)}, f32[3,1,1,4,256]{4,3,0,2,1:T(4,128)S(1)}, u32[]{:S(2)}, u32[]{:S(2)}) collective-permute-start(f32[3,1,1,4,256]{4,3,0,2,1:T(4,128)S(1)} %pad_maximum_fusion.3), channel_id=1, source_target_pairs={{256,0},{512,256},{768,512},{0,768},{257,1},{513,257},{769,513},{1... | collective-permute-start | bytes 36872 | tf_op jit(solution)/shard_map/ppermute | solution.py:20
  87.2 6.9 %collective-permute-done.9 = f32[3,1,1,4,256]{4,3,0,2,1:T(4,128)S(1)} collective-permute-done((f32[3,1,1,4,256]{4,3,0,2,1:T(4,128)S(1)}, f32[3,1,1,4,256]{4,3,0,2,1:T(4,128)S(1)}, u32[]{:S(2)}, u32[]{:S(2)}) %collective-permute-start.9) | collective-permute-done | bytes 12320 | tf_op jit(solution)/shard_map/ppermute | solution.py:20
  94.1 1.9 %collective-permute-start.10 = (f32[3,3,1,4,256]{4,3,0,2,1:T(4,128)S(1)}, f32[3,3,1,4,256]{4,3,0,2,1:T(4,128)S(1)}, u32[]{:S(2)}, u32[]{:S(2)}) collective-permute-start(f32[3,3,1,4,256]{4,3,0,2,1:T(4,128)S(1)} %pad_maximum_fusion.1), channel_id=1, source_target_pairs={{0,64},{64,128},{128,192},{192,0},{1,65},{65,129},{129,193},{193,1... | collective-permute-start | bytes 110600 | tf_op jit(solution)/shard_map/ppermute | solution.py:19
  96.0 5.9 %collective-permute-start.11 = (f32[3,3,1,4,256]{4,3,0,2,1:T(4,128)S(1)}, f32[3,3,1,4,256]{4,3,0,2,1:T(4,128)S(1)}, u32[]{:S(2)}, u32[]{:S(2)}) collective-permute-start(f32[3,3,1,4,256]{4,3,0,2,1:T(4,128)S(1)} %pad_maximum_fusion.1), channel_id=1, source_target_pairs={{64,0},{128,64},{192,128},{0,192},{65,1},{129,65},{193,129},{1,193... | collective-permute-start | bytes 110600 | tf_op jit(solution)/shard_map/ppermute | solution.py:20
  103.0 2.4 %fusion.56 = (f32[2,256,256]{2,1,0:T(8,128)S(1)}, f32[2,256,256]{2,1,0:T(8,128)S(1)}, f32[2,256,256]{2,1,0:T(8,128)S(1)}, f32[2,256,256]{2,1,0:T(8,128)S(1)}, f3...) fusion(f32[3,2,256]{2,1,0:T(2,128)S(1)} %get-tuple-element.137,, ...), kind=kLoop, calls=%fused_computation.164 | loop fusion | flops 10615296 | bytes 5316608 | tf_op jit(solution)/shard_map/reduce_sum | solution.py:53
  105.4 4.6 %fusion.57 = (f32[3,2,256]{2,1,0:T(2,128)S(1)}, f32[2,256,256]{2,1,0:T(8,128)S(1)}, f32[2,256,256]{2,1,0:T(8,128)S(1)}, f32[2,256,256]{2,1,0:T(8,128)S(1)}, f32[...) fusion(f32[2,256,256]{2,1,0:T(8,128)S(1)} %fusion.136, ...), kind=kLoop, calls=%fused_computation.165 | loop fusion | flops 19003904 | bytes 9553920 | tf_op jit(solution)/shard_map/reduce_sum | solution.py:56
  112.4 2.0 %fusion.63 = (f32[3,2,256]{2,1,0:T(2,128)S(1)}, f32[3,2,256]{2,1,0:T(2,128)S(1)}, f32[3,2,256]{2,1,0:T(2,128)S(1)}, f32[3,2,256]{2,1,0:T(2,128)S(1)}, f32[3,2,25...) fusion(f32[2,256,256]{2,1,0:T(8,128)S(1)} %fusion.139, ...), kind=kLoop, calls=%fused_computation.171 | loop fusion | flops 8246784 | bytes 3756032 | tf_op jit(solution)/shard_map/reduce_sum | solution.py:56
  114.4 2.4 %fusion.61 = (f32[3,2,256]{2,1,0:T(2,128)S(1)}, f32[3,2,256]{2,1,0:T(2,128)S(1)}, f32[3,2,256]{2,1,0:T(2,128)S(1)}, f32[3,2,256]{2,1,0:T(2,128)S(1)}, f32[3,2,25...) fusion(f32[2,256,256]{2,1,0:T(8,128)S(1)} %fusion.138, ...), kind=kLoop, calls=%fused_computation.169 | loop fusion | flops 10603008 | bytes 4835328 | tf_op jit(solution)/shard_map/reduce_sum | solution.py:56
  116.8 2.4 %fusion.59 = (f32[3,2,256]{2,1,0:T(2,128)S(1)}, f32[3,2,256]{2,1,0:T(2,128)S(1)}, f32[3,2,256]{2,1,0:T(2,128)S(1)}, f32[3,2,256]{2,1,0:T(2,128)S(1)}, f32[3,2,25...) fusion(f32[2,256,256]{2,1,0:T(8,128)S(1)} %fusion.137, ...), kind=kLoop, calls=%fused_computation.167 | loop fusion | flops 10603008 | bytes 4835328 | tf_op jit(solution)/shard_map/reduce_sum | solution.py:56
  (128 shorter events, 8.9 us)
Async XLA Ops:
  0.6 53.6 %copy-start = (f32[3,1,1,2,256]{4,3,2,1,0:T(2,128)S(1)}, f32[3,1,1,2,256]{4,3,2,1,0:T(2,128)}, u32[]{:S(2)}) copy-start(f32[3,1,1,2,256]{4,3,2,1,0:T(2,128)} %param.58) | copy-start | bytes 18436
  2.2 23.5 %collective-permute-start = (f32[4,1,1,1,256]{4,3,0,2,1:T(1,128)S(1)}, f32[4,1,1,1,256]{4,3,0,2,1:T(1,128)S(1)}, u32[]{:S(2)}, u32[]{:S(2)}) collective-permute-start(f32[4,1,1,1,256]{4,3,0,2,1:T(1,128)S(1)} %get-tuple-element.187), channel_id=1, source_target_pairs={{0,1},{1,2},{2,3},{3,4},{4,5},{5,6},{6,7},{7,8},{8,9},{9,10},{10,1... | collective-permute-start | bytes 12296 | tf_op jit(solution)/shard_map/ppermute | solution.py:19
  6.3 20.1 %collective-permute-start.1 = (f32[4,1,1,1,256]{4,3,0,2,1:T(1,128)S(1)}, f32[4,1,1,1,256]{4,3,0,2,1:T(1,128)S(1)}, u32[]{:S(2)}, u32[]{:S(2)}) collective-permute-start(f32[4,1,1,1,256]{4,3,0,2,1:T(1,128)S(1)} %get-tuple-element.188), channel_id=1, source_target_pairs={{1,0},{2,1},{3,2},{4,3},{5,4},{6,5},{7,6},{8,7},{9,8},{10,9},{11,1... | collective-permute-start | bytes 12296 | tf_op jit(solution)/shard_map/ppermute | solution.py:20
  27.1 11.3 %collective-permute-start.2 = (f32[4,1,1,4,256]{4,3,0,2,1:T(4,128)S(1)}, f32[4,1,1,4,256]{4,3,0,2,1:T(4,128)S(1)}, u32[]{:S(2)}, u32[]{:S(2)}) collective-permute-start(f32[4,1,1,4,256]{4,3,0,2,1:T(4,128)S(1)} %pad_maximum_fusion.2), channel_id=1, source_target_pairs={{0,256},{256,512},{512,768},{768,0},{1,257},{257,513},{513,769},{7... | collective-permute-start | bytes 49160 | tf_op jit(solution)/shard_map/ppermute | solution.py:19
  35.7 9.1 %collective-permute-start.3 = (f32[4,1,1,4,256]{4,3,0,2,1:T(4,128)S(1)}, f32[4,1,1,4,256]{4,3,0,2,1:T(4,128)S(1)}, u32[]{:S(2)}, u32[]{:S(2)}) collective-permute-start(f32[4,1,1,4,256]{4,3,0,2,1:T(4,128)S(1)} %pad_maximum_fusion.2), channel_id=1, source_target_pairs={{256,0},{512,256},{768,512},{0,768},{257,1},{513,257},{769,513},{1... | collective-permute-start | bytes 49160 | tf_op jit(solution)/shard_map/ppermute | solution.py:20
  45.5 8.6 %collective-permute-start.4 = (f32[4,3,1,4,256]{4,3,0,2,1:T(4,128)S(1)}, f32[4,3,1,4,256]{4,3,0,2,1:T(4,128)S(1)}, u32[]{:S(2)}, u32[]{:S(2)}) collective-permute-start(f32[4,3,1,4,256]{4,3,0,2,1:T(4,128)S(1)} %pad_maximum_fusion), channel_id=1, source_target_pairs={{0,64},{64,128},{128,192},{192,0},{1,65},{65,129},{129,193},{193,1... | collective-permute-start | bytes 147464 | tf_op jit(solution)/shard_map/ppermute | solution.py:19
  47.7 6.4 %collective-permute-start.5 = (f32[4,3,1,4,256]{4,3,0,2,1:T(4,128)S(1)}, f32[4,3,1,4,256]{4,3,0,2,1:T(4,128)S(1)}, u32[]{:S(2)}, u32[]{:S(2)}) collective-permute-start(f32[4,3,1,4,256]{4,3,0,2,1:T(4,128)S(1)} %pad_maximum_fusion), channel_id=1, source_target_pairs={{64,0},{128,64},{192,128},{0,192},{65,1},{129,65},{193,129},{1,193... | collective-permute-start | bytes 147464 | tf_op jit(solution)/shard_map/ppermute | solution.py:20
  54.6 0.7 copy-start.17
  54.6 0.8 copy-start.2
  54.6 0.8 copy-start.3
  54.7 0.8 copy-start.4
  54.7 0.8 copy-start.5
  54.7 0.8 copy-start.6
  54.7 0.8 copy-start.7
  54.7 0.8 copy-start.8
  54.7 0.8 copy-start.9
  69.3 2.5 %copy-start.1 = (f32[3,1,1,2,256]{4,3,2,1,0:T(2,128)S(1)}, f32[3,1,1,2,256]{4,3,2,1,0:T(2,128)}, u32[]{:S(2)}) copy-start(f32[3,1,1,2,256]{4,3,2,1,0:T(2,128)} %param.59) | copy-start | bytes 18436
  69.3 11.8 %copy-start.26 = (s32[1,1,2]{2,1,0:T(1,128)S(1)}, s32[1,1,2]{2,1,0:T(1,128)}, u32[]{:S(2)}) copy-start(s32[1,1,2]{2,1,0:T(1,128)} %param.61) | copy-start | bytes 28
  69.3 17.8 %copy-start.24 = (f32[3]{0:T(128)S(1)}, f32[3]{0:T(128)}, u32[]{:S(2)}) copy-start(f32[3]{0:T(128)} %constant.76.clone) | copy-start | bytes 40
  69.3 17.8 %copy-start.25 = (f32[3]{0:T(128)S(1)}, f32[3]{0:T(128)}, u32[]{:S(2)}) copy-start(f32[3]{0:T(128)} %constant.78.clone) | copy-start | bytes 40
  69.3 32.7 %copy-start.21 = (f32[3]{0:T(128)S(1)}, f32[3]{0:T(128)}, u32[]{:S(2)}) copy-start(f32[3]{0:T(128)} %constant.85.clone) | copy-start | bytes 40
  69.3 32.7 %copy-start.22 = (f32[3]{0:T(128)S(1)}, f32[3]{0:T(128)}, u32[]{:S(2)}) copy-start(f32[3]{0:T(128)} %constant.86.clone) | copy-start | bytes 40
  69.3 32.7 %copy-start.23 = (f32[3]{0:T(128)S(1)}, f32[3]{0:T(128)}, u32[]{:S(2)}) copy-start(f32[3]{0:T(128)} %constant.87.clone) | copy-start | bytes 40
  69.4 32.7 %copy-start.18 = (f32[3]{0:T(128)S(1)}, f32[3]{0:T(128)}, u32[]{:S(2)}) copy-start(f32[3]{0:T(128)} %constant.29.clone) | copy-start | bytes 40
  69.4 32.7 %copy-start.19 = (f32[3]{0:T(128)S(1)}, f32[3]{0:T(128)}, u32[]{:S(2)}) copy-start(f32[3]{0:T(128)} %constant.68.clone) | copy-start | bytes 40
  69.4 32.7 %copy-start.20 = (f32[3]{0:T(128)S(1)}, f32[3]{0:T(128)}, u32[]{:S(2)}) copy-start(f32[3]{0:T(128)} %constant.69.clone) | copy-start | bytes 40
  71.9 9.2 %collective-permute-start.6 = (f32[3,1,1,1,256]{4,3,0,2,1:T(1,128)S(1)}, f32[3,1,1,1,256]{4,3,0,2,1:T(1,128)S(1)}, u32[]{:S(2)}, u32[]{:S(2)}) collective-permute-start(f32[3,1,1,1,256]{4,3,0,2,1:T(1,128)S(1)} %get-tuple-element.191), channel_id=1, source_target_pairs={{0,1},{1,2},{2,3},{3,4},{4,5},{5,6},{6,7},{7,8},{8,9},{9,10},{10,1... | collective-permute-start | bytes 9224 | tf_op jit(solution)/shard_map/ppermute | solution.py:19
  73.8 8.0 %collective-permute-start.7 = (f32[3,1,1,1,256]{4,3,0,2,1:T(1,128)S(1)}, f32[3,1,1,1,256]{4,3,0,2,1:T(1,128)S(1)}, u32[]{:S(2)}, u32[]{:S(2)}) collective-permute-start(f32[3,1,1,1,256]{4,3,0,2,1:T(1,128)S(1)} %get-tuple-element.192), channel_id=1, source_target_pairs={{1,0},{2,1},{3,2},{4,3},{5,4},{6,5},{7,6},{8,7},{9,8},{10,9},{11,1... | collective-permute-start | bytes 9224 | tf_op jit(solution)/shard_map/ppermute | solution.py:20
  81.8 5.4 %collective-permute-start.8 = (f32[3,1,1,4,256]{4,3,0,2,1:T(4,128)S(1)}, f32[3,1,1,4,256]{4,3,0,2,1:T(4,128)S(1)}, u32[]{:S(2)}, u32[]{:S(2)}) collective-permute-start(f32[3,1,1,4,256]{4,3,0,2,1:T(4,128)S(1)} %pad_maximum_fusion.3), channel_id=1, source_target_pairs={{0,256},{256,512},{512,768},{768,0},{1,257},{257,513},{513,769},{7... | collective-permute-start | bytes 36872 | tf_op jit(solution)/shard_map/ppermute | solution.py:19
  85.2 8.9 %collective-permute-start.9 = (f32[3,1,1,4,256]{4,3,0,2,1:T(4,128)S(1)}, f32[3,1,1,4,256]{4,3,0,2,1:T(4,128)S(1)}, u32[]{:S(2)}, u32[]{:S(2)}) collective-permute-start(f32[3,1,1,4,256]{4,3,0,2,1:T(4,128)S(1)} %pad_maximum_fusion.3), channel_id=1, source_target_pairs={{256,0},{512,256},{768,512},{0,768},{257,1},{513,257},{769,513},{1... | collective-permute-start | bytes 36872 | tf_op jit(solution)/shard_map/ppermute | solution.py:20
  94.1 8.1 %collective-permute-start.10 = (f32[3,3,1,4,256]{4,3,0,2,1:T(4,128)S(1)}, f32[3,3,1,4,256]{4,3,0,2,1:T(4,128)S(1)}, u32[]{:S(2)}, u32[]{:S(2)}) collective-permute-start(f32[3,3,1,4,256]{4,3,0,2,1:T(4,128)S(1)} %pad_maximum_fusion.1), channel_id=1, source_target_pairs={{0,64},{64,128},{128,192},{192,0},{1,65},{65,129},{129,193},{193,1... | collective-permute-start | bytes 110600 | tf_op jit(solution)/shard_map/ppermute | solution.py:19
  96.0 6.8 %collective-permute-start.11 = (f32[3,3,1,4,256]{4,3,0,2,1:T(4,128)S(1)}, f32[3,3,1,4,256]{4,3,0,2,1:T(4,128)S(1)}, u32[]{:S(2)}, u32[]{:S(2)}) collective-permute-start(f32[3,3,1,4,256]{4,3,0,2,1:T(4,128)S(1)} %pad_maximum_fusion.1), channel_id=1, source_target_pairs={{64,0},{128,64},{192,128},{0,192},{65,1},{129,65},{193,129},{1,193... | collective-permute-start | bytes 110600 | tf_op jit(solution)/shard_map/ppermute | solution.py:20
  (7 other events, 4.7 us)
where the time goes:
time: 121 us; the launch traced here: 120 us
  starting transfers between devices  63.3 us (52%)
  other arithmetic  40.2 us (33%)
  waiting for transfers between devices  14.8 us (12%)
  between operations  1.64 us (1%)
    ppermute x6, starting transfers between devices, with_halo(): after = lax.ppermute(initial, axis, down)  41.2 us
    reduce_sum x8, other arithmetic, accelerations(): total = total + jnp.sum(delta * weighted[None], axis=-1)  22.6 us
    ppermute x6, starting transfers between devices, with_halo(): before = lax.ppermute(last, axis, up)  22.1 us
    ppermute x6, waiting for transfers between devices, with_halo(): after = lax.ppermute(initial, axis, down)  14.8 us
    reduce_sum x4, other arithmetic, accelerations(): squared = jnp.sum(delta * delta, axis=0)  5.31 us
    mul x42, other arithmetic, accelerations(): weighted = falloff * falloff * falloff * source_mass[:, None, :]  4.78 us
    add x14, other arithmetic, accelerations(): offset[:, None, None, None] + source[:, :, None, :]  3.01 us
  transfers between devices with their start and end apart: 12, of which 5 were waited for; matrix products, arithmetic and copies ran while one was open for 3% of the time, Pallas kernels for 0%

commit v1 on v0

v1 whole, which is shorter than its diff:
```python
import functools

import jax
import jax.numpy as jnp
from jax import lax
from jax.experimental import pallas as pl
from jax.experimental.pallas import tpu as pltpu
from jax.sharding import PartitionSpec as P

SUBCYCLES = 2
LANES = 128
time_step = 0.25
MESH = pl.DeviceIdType.MESH


def row_index():
    return lax.broadcasted_iota(jnp.int32, (8, LANES), 0)


def split(value):
    scaled = value * 65537.0
    high = scaled - (scaled - value)
    return high, value - high


def over_components(value):
    value = value + pltpu.roll(value, 2, 0)
    return value + pltpu.roll(value, 4, 0)


def frame_offset(row, offset_x, offset_y, offset_z):
    return jnp.where(row < 2, offset_x, jnp.where(row < 4, offset_y, jnp.where(row < 6, offset_z, 0.0)))


def source_features(packed, offset):
    row = row_index()
    is_mass = row >= 6
    moved = packed + offset
    high, low = split(moved)
    spatial = jnp.where(is_mass, 0.0, moved)
    norm = -over_components(spatial * spatial)
    norm_high, rest = split(norm)
    norm_mid, norm_low = split(rest)
    high = jnp.where(is_mass, 1.0, high)
    low = jnp.where(is_mass, 1.0, low)
    norm_mid, norm_low = pltpu.roll(norm_mid, 2, 0), pltpu.roll(norm_low, 4, 0)
    norms = jnp.where(row < 2, norm_high, jnp.where(row < 4, norm_mid, jnp.where(row < 6, norm_low, 0.0)))
    features = jnp.concatenate([high, low, high, norms], axis=0)
    mass = over_components(jnp.where(is_mass, packed, 0.0))
    moment_high, moment_low = split(mass * jnp.where(is_mass, 1.0, moved))
    even = row % 2 == 0
    moments = jnp.concatenate(
        [
            jnp.concatenate([jnp.where(even, part, 0.0), jnp.where(even, 0.0, part)], axis=1)
            for part in (moment_high, moment_low)
        ],
        axis=0,
    )
    return features.T.astype(jnp.bfloat16), moments.astype(jnp.bfloat16)


def target_features(packed, offset):
    row = row_index()
    is_mass = row >= 6
    even = row % 2 == 0
    moved = jnp.where(is_mass, 0.0, packed + offset)
    sides = [[], []]
    for half in range(2):
        mine = jnp.where(even, moved, pltpu.roll(moved, 1, 0)) if half == 0 else jnp.where(even, pltpu.roll(moved, 7, 0), moved)
        first, rest = split(1.0 - over_components(mine * mine))
        second, third = split(rest)
        high, low = split(2.0 * mine)
        stacked = jnp.concatenate(
            [
                jnp.where(is_mass, first, high),
                jnp.where(is_mass, second, high),
                jnp.where(is_mass, third, low),
                jnp.where(is_mass, 0.0, 1.0),
            ],
            axis=0,
        )
        parity = lax.broadcasted_iota(jnp.int32, (32, LANES), 0) % 2
        for source_half in range(2):
            sides[source_half].append(jnp.where(parity == source_half, stacked, 0.0))
    return jnp.concatenate(sides[0] + sides[1], axis=1).astype(jnp.bfloat16)


def pair_sums(features, moments, targets):
    falloff = jnp.maximum(jnp.dot(features, targets, preferred_element_type=jnp.float32), 0.0)
    weighted = falloff * falloff * falloff
    weighted = jnp.concatenate([weighted[:, : 2 * LANES], weighted[:, 2 * LANES :]], axis=0)
    high = weighted.astype(jnp.bfloat16)
    low = (weighted - high.astype(jnp.float32)).astype(jnp.bfloat16)
    return jnp.dot(moments, high, preferred_element_type=jnp.float32) + jnp.dot(
        moments, low, preferred_element_type=jnp.float32
    )


def packed_accel(total, packed, offset):
    row = row_index()
    even = row % 2 == 0
    folded = total[:8] + total[8:]
    halves = []
    for half in range(2):
        part = folded[:, half * LANES : (half + 1) * LANES]
        halves.append(jnp.where(even, part + pltpu.roll(part, 7, 0), part + pltpu.roll(part, 1, 0)))
    sums = jnp.where(even, halves[0], halves[1])
    mass_sum = over_components(jnp.where(row >= 6, sums, 0.0))
    return jnp.where(row >= 6, 0.0, sums - (packed + offset) * mass_sum)


def step_kernel(
    sizes, positions, velocities, mass, counts, new_positions, new_velocities, bins, targets, total, send_sem, recv_sem
):
    me = [lax.axis_index(name) for name in ("gx", "gy", "gz")]
    near = 1 - 2 * (me[0] % 2)

    def shift(xi, yi):
        return near * (xi % 2) - near * (xi // 2), (yi % 2) - (yi // 2)

    def neighbour(xi, yi, dz):
        dx, dy = shift(xi, yi)
        return tuple(lax.rem(at + d + size, size) for at, d, size in zip(me, (dx, dy, dz), sizes))

    peers = [
        (xi, yi, zi)
        for xi in (2, 1, 0)
        for yi in (1, 2, 0)
        for zi in (1, 2, 0)
        if (xi, yi, zi) != (0, 0, 0)
    ]
    shift_z = (0, 1, -1)

    barrier = pltpu.get_barrier_semaphore()
    for xi, yi, zi in peers:
        pl.semaphore_signal(barrier, inc=1, device_id=neighbour(xi, yi, shift_z[zi]), device_id_type=MESH)

    row = row_index()
    lane = lax.broadcasted_iota(jnp.int32, (8, LANES), 1)
    slot = lane + LANES * (row % 2)
    occupied = [slot < counts[0, 0, b] for b in range(2)]
    speed = []
    for b in range(2):
        place_rows = [positions[c, 0, 0, b : b + 1, h * LANES : (h + 1) * LANES] for c in range(3) for h in range(2)]
        mass_rows = [mass[0, 0, b : b + 1, h * LANES : (h + 1) * LANES] for h in range(2)]
        packed = jnp.concatenate(place_rows + mass_rows, axis=0)
        bins[0, 0, 1 + b] = jnp.where((row < 6) | occupied[b], packed, 0.0)
        speed_rows = [velocities[c, 0, 0, b : b + 1, h * LANES : (h + 1) * LANES] for c in range(3) for h in range(2)]
        speed.append(jnp.concatenate(speed_rows + [jnp.zeros((2, LANES), jnp.float32)], axis=0))

    pl.semaphore_wait(barrier, len(peers))

    copies = []
    for sub in range(SUBCYCLES):
        for xi, yi, zi in peers:
            from_them = xi * 3 + (3 - yi) % 3
            source = bins.at[sub, 0, pl.ds(1, 2)] if zi == 0 else bins.at[sub, 0, pl.ds(2 if zi == 1 else 1, 1)]
            target = bins.at[sub, from_them, pl.ds(1, 2)] if zi == 0 else bins.at[sub, from_them, pl.ds(0 if zi == 1 else 3, 1)]
            copy = pltpu.make_async_remote_copy(
                src_ref=source,
                dst_ref=target,
                send_sem=send_sem.at[sub, from_them, zi],
                recv_sem=recv_sem.at[sub, from_them, zi],
                device_id=neighbour(xi, yi, shift_z[zi]),
                device_id_type=MESH,
            )
            copy.start()
            copies.append(copy)

        for b in range(2):
            targets[b] = target_features(bins[sub, 0, 1 + b], frame_offset(row, -0.5, -0.5, b - 1.0))
        total[...] = jnp.zeros_like(total)

        def arrived(column, zi):
            width = 2 if zi == 0 else 1
            place = bins.at[sub, column, pl.ds((1, 0, 3)[zi], width)]
            pltpu.make_async_remote_copy(
                src_ref=place,
                dst_ref=place,
                send_sem=send_sem.at[sub, column, zi],
                recv_sem=recv_sem.at[sub, column, zi],
                device_id=neighbour(0, 0, 1),
                device_id_type=MESH,
            ).wait_recv()

        def column_sums(column):
            dx, dy = shift(column // 3, column % 3)
            offset_x = dx.astype(jnp.float32) - 0.5
            offset_y = dy.astype(jnp.float32) - 0.5
            sums = [None, None]
            for z in range(4):
                features, moments = source_features(
                    bins[sub, column, z], frame_offset(row, offset_x, offset_y, z - 2.0)
                )
                for b in range(2):
                    if abs(z - 1 - b) <= 1:
                        value = pair_sums(features, moments, targets[b])
                        sums[b] = value if sums[b] is None else sums[b] + value
            for b in range(2):
                total[b] += sums[b]

        arrived(0, 1)
        arrived(0, 2)
        column_sums(jnp.int32(0))

        def body(column, carry):
            for zi in range(3):
                arrived(column, zi)
            column_sums(column)
            return carry

        lax.fori_loop(1, 9, body, 0)

        for b in range(2):
            packed = bins[sub, 0, 1 + b]
            accel = packed_accel(total[b], packed, frame_offset(row, -0.5, -0.5, b - 1.0))
            speed[b] = speed[b] + time_step * accel
            moved = jnp.clip(packed + time_step * speed[b], 0.0, 1.0)
            if sub + 1 < SUBCYCLES:
                bins[sub + 1, 0, 1 + b] = jnp.where(row < 6, moved, packed)
            else:
                moved = jnp.where(occupied[b], moved, 0.0)
                final_speed = jnp.where(occupied[b], speed[b], 0.0)
                for c in range(3):
                    for h in range(2):
                        r = 2 * c + h
                        new_positions[c, 0, 0, b : b + 1, h * LANES : (h + 1) * LANES] = moved[r : r + 1]
                        new_velocities[c, 0, 0, b : b + 1, h * LANES : (h + 1) * LANES] = final_speed[r : r + 1]

    for copy in copies:
        copy.wait_send()


def solution(mesh):
    placed = (
        P(None, "gx", "gy", "gz", None),
        P(None, "gx", "gy", "gz", None),
        P("gx", "gy", "gz", None),
        P("gx", "gy", "gz"),
    )
    sizes = tuple(mesh.shape[name] for name in ("gx", "gy", "gz"))

    def on_device(positions, velocities, mass, counts):
        vmem = pl.BlockSpec(memory_space=pltpu.VMEM)
        return pl.pallas_call(
            functools.partial(step_kernel, sizes),
            out_shape=(
                jax.ShapeDtypeStruct(positions.shape, jnp.float32),
                jax.ShapeDtypeStruct(velocities.shape, jnp.float32),
            ),
            in_specs=[vmem, vmem, vmem, pl.BlockSpec(memory_space=pltpu.SMEM)],
            out_specs=(vmem, vmem),
            scratch_shapes=[
                pltpu.VMEM((SUBCYCLES, 9, 4, 8, LANES), jnp.float32),
                pltpu.VMEM((2, 32, 4 * LANES), jnp.bfloat16),
                pltpu.VMEM((2, 16, 2 * LANES), jnp.float32),
                pltpu.SemaphoreType.DMA((SUBCYCLES, 9, 3)),
                pltpu.SemaphoreType.DMA((SUBCYCLES, 9, 3)),
            ],
            compiler_params=pltpu.CompilerParams(collective_id=0, has_side_effects=True),
        )(positions, velocities, mass, counts)

    return jax.shard_map(
        on_device,
        mesh=mesh,
        in_specs=placed,
        out_specs=(P(None, "gx", "gy", "gz", None), P(None, "gx", "gy", "gz", None)),
        check_vma=False,
    )
```

time: 121 us -> 57.8 us (0.48)
  starting transfers between devices: 63.3 us -> 0 us
  Pallas kernels: 0 us -> 55 us
  other arithmetic: 40.2 us -> 0 us
  waiting for transfers between devices: 14.8 us -> 0 us
  local copies, waits for them, and re-layouts: 0.65 us -> 1.89 us
    ppermute x12 -> x0, starting transfers between devices: 63.3 us -> none  [the longest x6 41.2 us: with_halo(): after = lax.ppermute(initial, axis, down)]
    pallas_call x0 -> x1, Pallas kernels: none -> 55 us  [on_device(): pl.pallas_call(functools.partial(step_kernel, sizes), out_shape=(jax.Shap...]
    reduce_sum x12 -> x0, other arithmetic: 27.9 us -> none  [the longest x8 22.6 us: accelerations(): total = total + jnp.sum(delta * weighted[None], axis=-1)]
    ppermute x12 -> x0, waiting for transfers between devices: 14.8 us -> none  [the longest x6 14.8 us: with_halo(): after = lax.ppermute(initial, axis, down)]
    mul x42 -> x0, other arithmetic: 4.78 us -> none  [accelerations(): weighted = falloff * falloff * falloff * source_mass[:, None, :]]
    add x14 -> x0, other arithmetic: 3.01 us -> none  [accelerations(): offset[:, None, None, None] + source[:, :, None, :]]
    concatenate x5 -> x0, other arithmetic: 2.23 us -> none  [the longest x4 1.45 us: with_halo(): array = jnp.concatenate([before, array, after], axis=dim)]
    unnamed x2 -> x0, other arithmetic: 1.28 us -> none
  transfers between devices with their start and end apart: 12 -> 0, of which waited for: 5 -> 0; matrix products, arithmetic and copies ran while one was open for 3% -> 0% of each run, Pallas kernels for 0% -> 0%
where the time goes in v1:
time: 57.8 us; the launch traced here: 57.5 us
  Pallas kernels  55 us (95%)
  local copies, waits for them, and re-layouts  1.89 us (3%)
  between operations  0.65 us (1%)
    pallas_call x1, Pallas kernels, on_device(): pl.pallas_call(functools.partial(step_kernel, sizes), out_shape=(jax.Shap...  55 us
    unnamed x4, local copies, waits for them, and re-layouts  1.89 us

profile of v1, /device:TPU:1, one launch (start us, length us, event | category | flops | bytes accessed | tf_op | source)
XLA Modules:
  0.0 57.5 jit_solution(1885961046574242341)
XLA Ops:
  0.6 55.0 %shard_map.59 = (f32[3,1,1,2,256]{4,3,2,1,0:T(2,128)}, f32[3,1,1,2,256]{4,3,2,1,0:T(2,128)}) custom-call(f32[3,1,1,2,256]{4,3,2,1,0:T(2,128)} %positions.1, f32[3,1,1,2,256]{4,3,2,1,0:T(2,128)} %velocities.1, f32[1,1,2,256]{3,2,1,0:T(2,128)} %mass.1, s32[1,1,2]{2,1,0:T(1,128)} %counts.1), custom_call_target="tpu_custom_call" | custom-call | tf_op jit(solution)/shard_map/pallas_call | solution.py:245
  55.6 0.0 copy-start
  55.7 1.3 %copy.8 = f32[3,1,1,2,256]{4,3,2,1,0:T(2,128)} copy(f32[3,1,1,2,256]{4,3,2,1,0:T(2,128)} %get-tuple-element.4) | data formatting | bytes 12288
  56.9 0.0 copy-done
  57.0 0.6 %copy.9 = f32[3,1,1,2,256]{4,3,2,1,0:T(2,128)} copy(f32[3,1,1,2,256]{4,3,2,1,0:T(2,128)S(1)} %copy-done) | data formatting | bytes 12288
Async XLA Ops:
  55.6 1.3 %copy-start = (f32[3,1,1,2,256]{4,3,2,1,0:T(2,128)S(1)}, f32[3,1,1,2,256]{4,3,2,1,0:T(2,128)}, u32[]{:S(2)}) copy-start(f32[3,1,1,2,256]{4,3,2,1,0:T(2,128)} %get-tuple-element.5) | copy-start | bytes 18436

commit v2 on v1

--- a/solution.py
+++ b/solution.py
@@ -9,6 +9,12 @@
 
 SUBCYCLES = 2
 LANES = 128
+GROUPS = (
+    ((0, 1),),
+    ((1, 1),),
+    ((2, 1), (3, 1), (4, 1), (5, 1), (0, 0), (1, 0)),
+    ((6, 1), (7, 1), (8, 1), (2, 0), (3, 0), (4, 0), (5, 0), (6, 0), (7, 0), (8, 0)),
+)
 time_step = 0.25
 MESH = pl.DeviceIdType.MESH
 
@@ -110,70 +116,84 @@
 
 
 def step_kernel(
-    sizes, positions, velocities, mass, counts, new_positions, new_velocities, bins, targets, total, send_sem, recv_sem
+    sizes,
+    positions,
+    velocities,
+    mass,
+    counts,
+    moved_out,
+    place_in,
+    speed_in,
+    mass_in,
+    count_in,
+    bins,
+    targets,
+    total,
+    input_sem,
+    send_sem,
+    recv_sem,
 ):
+    inputs = [
+        pltpu.make_async_copy(source, target, input_sem.at[i])
+        for i, (source, target) in enumerate(
+            ((positions, place_in), (mass, mass_in), (counts, count_in), (velocities, speed_in))
+        )
+    ]
+    for load in inputs:
+        load.start()
+
     me = [lax.axis_index(name) for name in ("gx", "gy", "gz")]
     near = 1 - 2 * (me[0] % 2)
-
-    def shift(xi, yi):
-        return near * (xi % 2) - near * (xi // 2), (yi % 2) - (yi // 2)
-
-    def neighbour(xi, yi, dz):
-        dx, dy = shift(xi, yi)
-        return tuple(lax.rem(at + d + size, size) for at, d, size in zip(me, (dx, dy, dz), sizes))
-
-    peers = [
-        (xi, yi, zi)
-        for xi in (2, 1, 0)
-        for yi in (1, 2, 0)
-        for zi in (1, 2, 0)
-        if (xi, yi, zi) != (0, 0, 0)
-    ]
     shift_z = (0, 1, -1)
 
+    def neighbour(xi, yi, zi):
+        dx = near * (xi % 2) - near * (xi // 2)
+        dy = (yi % 2) - (yi // 2)
+        return tuple(lax.rem(at + d + size, size) for at, d, size in zip(me, (dx, dy, shift_z[zi]), sizes))
+
+    order = ((0, 0), (1, 0), (0, 1), (0, 2), (1, 1), (1, 2), (2, 1), (2, 2), (2, 0))
+    peers = [(xi, yi, zi) for xi, yi in reversed(order) for zi in range(3) if (xi, yi, zi) != (0, 0, 0)]
+
     barrier = pltpu.get_barrier_semaphore()
-    for xi, yi, zi in peers:
-        pl.semaphore_signal(barrier, inc=1, device_id=neighbour(xi, yi, shift_z[zi]), device_id_type=MESH)
+    for peer in peers:
+        pl.semaphore_signal(barrier, inc=1, device_id=neighbour(*peer), device_id_type=MESH)
 
     row = row_index()
     lane = lax.broadcasted_iota(jnp.int32, (8, LANES), 1)
     slot = lane + LANES * (row % 2)
-    occupied = [slot < counts[0, 0, b] for b in range(2)]
+    own_offset = [frame_offset(row, -0.5, -0.5, b - 1.0) for b in range(2)]
+    for load in inputs:
+        load.wait()
     speed = []
     for b in range(2):
-        place_rows = [positions[c, 0, 0, b : b + 1, h * LANES : (h + 1) * LANES] for c in range(3) for h in range(2)]
-        mass_rows = [mass[0, 0, b : b + 1, h * LANES : (h + 1) * LANES] for h in range(2)]
+        place_rows = [place_in[c, 0, 0, b : b + 1, h * LANES : (h + 1) * LANES] for c in range(3) for h in range(2)]
+        mass_rows = [mass_in[0, 0, b : b + 1, h * LANES : (h + 1) * LANES] for h in range(2)]
         packed = jnp.concatenate(place_rows + mass_rows, axis=0)
-        bins[0, 0, 1 + b] = jnp.where((row < 6) | occupied[b], packed, 0.0)
-        speed_rows = [velocities[c, 0, 0, b : b + 1, h * LANES : (h + 1) * LANES] for c in range(3) for h in range(2)]
+        bins[0, 0, 1 + b] = jnp.where((row < 6) | (slot < count_in[0, 0, b]), packed, 0.0)
+        speed_rows = [speed_in[c, 0, 0, b : b + 1, h * LANES : (h + 1) * LANES] for c in range(3) for h in range(2)]
         speed.append(jnp.concatenate(speed_rows + [jnp.zeros((2, LANES), jnp.float32)], axis=0))
-
-    pl.semaphore_wait(barrier, len(peers))
 
     copies = []
     for sub in range(SUBCYCLES):
-        for xi, yi, zi in peers:
-            from_them = xi * 3 + (3 - yi) % 3
-            source = bins.at[sub, 0, pl.ds(1, 2)] if zi == 0 else bins.at[sub, 0, pl.ds(2 if zi == 1 else 1, 1)]
-            target = bins.at[sub, from_them, pl.ds(1, 2)] if zi == 0 else bins.at[sub, from_them, pl.ds(0 if zi == 1 else 3, 1)]
-            copy = pltpu.make_async_remote_copy(
-                src_ref=source,
-                dst_ref=target,
-                send_sem=send_sem.at[sub, from_them, zi],
-                recv_sem=recv_sem.at[sub, from_them, zi],
-                device_id=neighbour(xi, yi, shift_z[zi]),
-                device_id_type=MESH,
-            )
-            copy.start()
-            copies.append(copy)
-
-        for b in range(2):
-            targets[b] = target_features(bins[sub, 0, 1 + b], frame_offset(row, -0.5, -0.5, b - 1.0))
-        total[...] = jnp.zeros_like(total)
+
+        def send():
+            for xi, yi, zi in peers:
+                column = order.index((xi, (3 - yi) % 3))
+                source = bins.at[sub, 0, pl.ds((1, 2, 1)[zi], 2 if zi == 0 else 1)]
+                target = bins.at[sub, column, pl.ds((1, 0, 3)[zi], 2 if zi == 0 else 1)]
+                copy = pltpu.make_async_remote_copy(
+                    src_ref=source,
+                    dst_ref=target,
+                    send_sem=send_sem.at[sub, column, zi],
+                    recv_sem=recv_sem.at[sub, column, zi],
+                    device_id=neighbour(xi, yi, zi),
+                    device_id_type=MESH,
+                )
+                copy.start()
+                copies.append(copy)
 
         def arrived(column, zi):
-            width = 2 if zi == 0 else 1
-            place = bins.at[sub, column, pl.ds((1, 0, 3)[zi], width)]
+            place = bins.at[sub, column, pl.ds((1, 0, 3)[zi], 2 if zi == 0 else 1)]
             pltpu.make_async_remote_copy(
                 src_ref=place,
                 dst_ref=place,
@@ -183,12 +203,12 @@
                 device_id_type=MESH,
             ).wait_recv()
 
-        def column_sums(column):
-            dx, dy = shift(column // 3, column % 3)
-            offset_x = dx.astype(jnp.float32) - 0.5
-            offset_y = dy.astype(jnp.float32) - 0.5
-            sums = [None, None]
-            for z in range(4):
+        def column_sums(column, slots, sums):
+            xi, yi = order[column]
+            offset_x = (near * (xi % 2) - near * (xi // 2)).astype(jnp.float32) - 0.5 if xi else -0.5
+            offset_y = float((yi % 2) - (yi // 2)) - 0.5
+            sums = list(sums)
+            for z in slots:
                 features, moments = source_features(
                     bins[sub, column, z], frame_offset(row, offset_x, offset_y, z - 2.0)
                 )
@@ -196,36 +216,50 @@
                     if abs(z - 1 - b) <= 1:
                         value = pair_sums(features, moments, targets[b])
                         sums[b] = value if sums[b] is None else sums[b] + value
+            return sums
+
+        def accumulate(group):
+            for column, inner in group:
+                for zi in (0,) if inner else (1, 2):
+                    if (column, zi) != (0, 0):
+                        arrived(column, zi)
+            sums = [None, None]
+            for column, inner in group:
+                sums = column_sums(column, (1, 2) if inner else (0, 3), sums)
             for b in range(2):
                 total[b] += sums[b]
 
-        arrived(0, 1)
-        arrived(0, 2)
-        column_sums(jnp.int32(0))
-
-        def body(column, carry):
-            for zi in range(3):
-                arrived(column, zi)
-            column_sums(column)
-            return carry
-
-        lax.fori_loop(1, 9, body, 0)
+        if sub == 0:
+            for b in range(2):
+                targets[b] = target_features(bins[sub, 0, 1 + b], own_offset[b])
+            total[...] = jnp.zeros_like(total)
+            pl.semaphore_wait(barrier, len(peers))
+            send()
+        else:
+            send()
+            for b in range(2):
+                targets[b] = target_features(bins[sub, 0, 1 + b], own_offset[b])
+            total[...] = jnp.zeros_like(total)
+
+        for group in GROUPS:
+            accumulate(group)
 
         for b in range(2):
             packed = bins[sub, 0, 1 + b]
-            accel = packed_accel(total[b], packed, frame_offset(row, -0.5, -0.5, b - 1.0))
+            accel = packed_accel(total[b], packed, own_offset[b])
             speed[b] = speed[b] + time_step * accel
             moved = jnp.clip(packed + time_step * speed[b], 0.0, 1.0)
             if sub + 1 < SUBCYCLES:
                 bins[sub + 1, 0, 1 + b] = jnp.where(row < 6, moved, packed)
             else:
-                moved = jnp.where(occupied[b], moved, 0.0)
-                final_speed = jnp.where(occupied[b], speed[b], 0.0)
+                occupied = slot < count_in[0, 0, b]
+                moved = jnp.where(occupied, moved, 0.0)
+                final_speed = jnp.where(occupied, speed[b], 0.0)
                 for c in range(3):
                     for h in range(2):
                         r = 2 * c + h
-                        new_positions[c, 0, 0, b : b + 1, h * LANES : (h + 1) * LANES] = moved[r : r + 1]
-                        new_velocities[c, 0, 0, b : b + 1, h * LANES : (h + 1) * LANES] = final_speed[r : r + 1]
+                        moved_out[c, 0, 0, b : b + 1, h * LANES : (h + 1) * LANES] = moved[r : r + 1]
+                        moved_out[3 + c, 0, 0, b : b + 1, h * LANES : (h + 1) * LANES] = final_speed[r : r + 1]
 
     for copy in copies:
         copy.wait_send()
@@ -241,24 +275,27 @@
     sizes = tuple(mesh.shape[name] for name in ("gx", "gy", "gz"))
 
     def on_device(positions, velocities, mass, counts):
-        vmem = pl.BlockSpec(memory_space=pltpu.VMEM)
-        return pl.pallas_call(
+        anywhere = pl.BlockSpec(memory_space=pl.ANY)
+        moved = pl.pallas_call(
             functools.partial(step_kernel, sizes),
-            out_shape=(
-                jax.ShapeDtypeStruct(positions.shape, jnp.float32),
-                jax.ShapeDtypeStruct(velocities.shape, jnp.float32),
-            ),
-            in_specs=[vmem, vmem, vmem, pl.BlockSpec(memory_space=pltpu.SMEM)],
-            out_specs=(vmem, vmem),
+            out_shape=jax.ShapeDtypeStruct((6,) + positions.shape[1:], jnp.float32),
+            in_specs=[anywhere] * 4,
+            out_specs=pl.BlockSpec(memory_space=pltpu.VMEM),
             scratch_shapes=[
+                pltpu.VMEM(positions.shape, jnp.float32),
+                pltpu.VMEM(velocities.shape, jnp.float32),
+                pltpu.VMEM(mass.shape, jnp.float32),
+                pltpu.SMEM(counts.shape, jnp.int32),
                 pltpu.VMEM((SUBCYCLES, 9, 4, 8, LANES), jnp.float32),
                 pltpu.VMEM((2, 32, 4 * LANES), jnp.bfloat16),
                 pltpu.VMEM((2, 16, 2 * LANES), jnp.float32),
+                pltpu.SemaphoreType.DMA((4,)),
                 pltpu.SemaphoreType.DMA((SUBCYCLES, 9, 3)),
                 pltpu.SemaphoreType.DMA((SUBCYCLES, 9, 3)),
             ],
             compiler_params=pltpu.CompilerParams(collective_id=0, has_side_effects=True),
         )(positions, velocities, mass, counts)
+        return moved[:3], moved[3:]
 
     return jax.shard_map(
         on_device,

time: 57.8 us -> 48.2 us (0.83)
  Pallas kernels: 55 us -> 46.1 us
  local copies, waits for them, and re-layouts: 1.89 us -> 1.31 us
    pallas_call x1, Pallas kernels: 55 us -> 46.1 us  [on_device(): pl.pallas_call(functools.partial(step_kernel, sizes), out_shape=jax.Shape...]
    unnamed x4 -> x0, local copies, waits for them, and re-layouts: 1.89 us -> none
    slice x0 -> x1, local copies, waits for them, and re-layouts: none -> 1.31 us  [on_device(): return (moved[:3], moved[3:])]
where the time goes in v2:
time: 48.2 us; the launch traced here: 48 us
  Pallas kernels  46.1 us (96%)
  local copies, waits for them, and re-layouts  1.31 us (3%)
  between operations  0.64 us (1%)
    pallas_call x1, Pallas kernels, on_device(): pl.pallas_call(functools.partial(step_kernel, sizes), out_shape=jax.Shape...  46.1 us
    slice x1, local copies, waits for them, and re-layouts, on_device(): return (moved[:3], moved[3:])  1.31 us

profile of v2, /device:TPU:1, one launch (start us, length us, event | category | flops | bytes accessed | tf_op | source)
XLA Modules:
  0.0 48.0 jit_solution(7779942187558618243)
XLA Ops:
  0.6 46.1 %shard_map.59 = f32[6,1,1,2,256]{4,3,2,1,0:T(2,128)} custom-call(f32[3,1,1,2,256]{4,3,2,1,0:T(2,128)} %positions.1, f32[3,1,1,2,256]{4,3,2,1,0:T(2,128)} %velocities.1, f32[1,1,2,256]{3,2,1,0:T(2,128)} %mass.1, s32[1,1,2]{2,1,0:T(1,128)} %counts.1), custom_call_target="tpu_custom_call" | custom-call | tf_op jit(solution)/shard_map/pallas_call | solution.py:279
  46.7 1.3 %fusion = (f32[3,1,1,2,256]{4,3,2,1,0:T(2,128)}, f32[3,1,1,2,256]{4,3,2,1,0:T(2,128)}) fusion(f32[6,1,1,2,256]{4,3,2,1,0:T(2,128)} %shard_map.59), kind=kLoop, calls=%fused_computation | loop fusion | bytes 24576 | tf_op jit(solution)/shard_map/slice | solution.py:298

commit v3 on v2

--- a/solution.py
+++ b/solution.py
@@ -11,8 +11,7 @@
 LANES = 128
 GROUPS = (
     ((0, 1),),
-    ((1, 1),),
-    ((2, 1), (3, 1), (4, 1), (5, 1), (0, 0), (1, 0)),
+    ((1, 1), (2, 1), (3, 1), (4, 1), (5, 1), (0, 0), (1, 0)),
     ((6, 1), (7, 1), (8, 1), (2, 0), (3, 0), (4, 0), (5, 0), (6, 0), (7, 0), (8, 0)),
 )
 time_step = 0.25
@@ -233,6 +232,7 @@
             for b in range(2):
                 targets[b] = target_features(bins[sub, 0, 1 + b], own_offset[b])
             total[...] = jnp.zeros_like(total)
+            accumulate(GROUPS[0])
             pl.semaphore_wait(barrier, len(peers))
             send()
         else:
@@ -240,8 +240,9 @@
             for b in range(2):
                 targets[b] = target_features(bins[sub, 0, 1 + b], own_offset[b])
             total[...] = jnp.zeros_like(total)
-
-        for group in GROUPS:
+            accumulate(GROUPS[0])
+
+        for group in GROUPS[1:]:
             accumulate(group)
 
         for b in range(2):
@@ -278,7 +279,7 @@
         anywhere = pl.BlockSpec(memory_space=pl.ANY)
         moved = pl.pallas_call(
             functools.partial(step_kernel, sizes),
-            out_shape=jax.ShapeDtypeStruct((6,) + positions.shape[1:], jnp.float32),
+            out_shape=pltpu.VMEM((6,) + positions.shape[1:], jnp.float32),
             in_specs=[anywhere] * 4,
             out_specs=pl.BlockSpec(memory_space=pltpu.VMEM),
             scratch_shapes=[

time: 48.2 us -> 46.9 us (0.973)
  local copies, waits for them, and re-layouts: 1.31 us -> 0.6 us
  Pallas kernels: 46.1 us -> 45.5 us
    slice x1, local copies, waits for them, and re-layouts: 1.31 us -> 0.6 us  [on_device(): return (moved[:3], moved[3:])]
    pallas_call x1, Pallas kernels: 46.1 us -> 45.5 us  [on_device(): pl.pallas_call(functools.partial(step_kernel, sizes), out_shape=pltpu.VME...]
where the time goes in v3:
time: 46.9 us; the launch traced here: 46.7 us
  Pallas kernels  45.5 us (97%)
  between operations  0.64 us (1%)
  local copies, waits for them, and re-layouts  0.6 us (1%)
    pallas_call x1, Pallas kernels, on_device(): pl.pallas_call(functools.partial(step_kernel, sizes), out_shape=pltpu.VME...  45.5 us

profile of v3, /device:TPU:1, one launch (start us, length us, event | category | flops | bytes accessed | tf_op | source)
XLA Modules:
  0.0 46.7 jit_solution(9447860425719678567)
XLA Ops:
  0.6 45.5 %shard_map.59 = f32[6,1,1,2,256]{4,3,2,1,0:T(2,128)S(1)} custom-call(f32[3,1,1,2,256]{4,3,2,1,0:T(2,128)} %positions.1, f32[3,1,1,2,256]{4,3,2,1,0:T(2,128)} %velocities.1, f32[1,1,2,256]{3,2,1,0:T(2,128)} %mass.1, s32[1,1,2]{2,1,0:T(1,128)} %counts.1), custom_call_target="tpu_custom_call" | custom-call | tf_op jit(solution)/shard_map/pallas_call | solution.py:280
  46.1 0.6 %fusion = (f32[3,1,1,2,256]{4,3,2,1,0:T(2,128)}, f32[3,1,1,2,256]{4,3,2,1,0:T(2,128)}) fusion(f32[6,1,1,2,256]{4,3,2,1,0:T(2,128)S(1)} %shard_map.59), kind=kLoop, calls=%fused_computation | loop fusion | bytes 24576 | tf_op jit(solution)/shard_map/slice | solution.py:299

commit v4 on v3

--- a/solution.py
+++ b/solution.py
@@ -178,8 +178,9 @@
         def send():
             for xi, yi, zi in peers:
                 column = order.index((xi, (3 - yi) % 3))
-                source = bins.at[sub, 0, pl.ds((1, 2, 1)[zi], 2 if zi == 0 else 1)]
-                target = bins.at[sub, column, pl.ds((1, 0, 3)[zi], 2 if zi == 0 else 1)]
+                rows = pl.ds(0, 8 if sub == 0 else 6)
+                source = bins.at[sub, 0, pl.ds((1, 2, 1)[zi], 2 if zi == 0 else 1), rows]
+                target = bins.at[sub, column, pl.ds((1, 0, 3)[zi], 2 if zi == 0 else 1), rows]
                 copy = pltpu.make_async_remote_copy(
                     src_ref=source,
                     dst_ref=target,
@@ -192,7 +193,7 @@
                 copies.append(copy)
 
         def arrived(column, zi):
-            place = bins.at[sub, column, pl.ds((1, 0, 3)[zi], 2 if zi == 0 else 1)]
+            place = bins.at[sub, column, pl.ds((1, 0, 3)[zi], 2 if zi == 0 else 1), pl.ds(0, 8 if sub == 0 else 6)]
             pltpu.make_async_remote_copy(
                 src_ref=place,
                 dst_ref=place,
@@ -208,9 +209,10 @@
             offset_y = float((yi % 2) - (yi // 2)) - 0.5
             sums = list(sums)
             for z in slots:
-                features, moments = source_features(
-                    bins[sub, column, z], frame_offset(row, offset_x, offset_y, z - 2.0)
-                )
+                packed = bins[sub, column, z]
+                if sub > 0:
+                    packed = jnp.where(row < 6, packed, bins[0, column, z])
+                features, moments = source_features(packed, frame_offset(row, offset_x, offset_y, z - 2.0))
                 for b in range(2):
                     if abs(z - 1 - b) <= 1:
                         value = pair_sums(features, moments, targets[b])

time: 46.9 us -> 46.6 us (level)
  no operation moved by 1% of the time
where the time goes in v4:
time: 46.6 us; the launch traced here: 46.5 us
  Pallas kernels  45.2 us (97%)
  between operations  0.64 us (1%)
  local copies, waits for them, and re-layouts  0.6 us (1%)
    pallas_call x1, Pallas kernels, on_device(): pl.pallas_call(functools.partial(step_kernel, sizes), out_shape=pltpu.VME...  45.2 us

profile of v4, /device:TPU:1, one launch (start us, length us, event | category | flops | bytes accessed | tf_op | source)
XLA Modules:
  0.0 46.5 jit_solution(12621256766086415437)
XLA Ops:
  0.6 45.2 %shard_map.59 = f32[6,1,1,2,256]{4,3,2,1,0:T(2,128)S(1)} custom-call(f32[3,1,1,2,256]{4,3,2,1,0:T(2,128)} %positions.1, f32[3,1,1,2,256]{4,3,2,1,0:T(2,128)} %velocities.1, f32[1,1,2,256]{3,2,1,0:T(2,128)} %mass.1, s32[1,1,2]{2,1,0:T(1,128)} %counts.1), custom_call_target="tpu_custom_call" | custom-call | tf_op jit(solution)/shard_map/pallas_call | solution.py:282
  45.9 0.6 %fusion = (f32[3,1,1,2,256]{4,3,2,1,0:T(2,128)}, f32[3,1,1,2,256]{4,3,2,1,0:T(2,128)}) fusion(f32[6,1,1,2,256]{4,3,2,1,0:T(2,128)S(1)} %shard_map.59), kind=kLoop, calls=%fused_computation | loop fusion | bytes 24576 | tf_op jit(solution)/shard_map/slice | solution.py:301

commit v5 on v4

--- a/solution.py
+++ b/solution.py
@@ -11,8 +11,9 @@
 LANES = 128
 GROUPS = (
     ((0, 1),),
-    ((1, 1), (2, 1), (3, 1), (4, 1), (5, 1), (0, 0), (1, 0)),
-    ((6, 1), (7, 1), (8, 1), (2, 0), (3, 0), (4, 0), (5, 0), (6, 0), (7, 0), (8, 0)),
+    ((1, 1), (2, 1), (3, 1)),
+    ((4, 1), (5, 1), (0, 0), (1, 0), (2, 0), (3, 0)),
+    ((6, 1), (7, 1), (8, 1), (4, 0), (5, 0), (6, 0), (7, 0), (8, 0)),
 )
 time_step = 0.25
 MESH = pl.DeviceIdType.MESH
@@ -143,14 +144,15 @@
 
     me = [lax.axis_index(name) for name in ("gx", "gy", "gz")]
     near = 1 - 2 * (me[0] % 2)
+    near_y = 1 - 2 * (me[1] % 2)
     shift_z = (0, 1, -1)
 
     def neighbour(xi, yi, zi):
         dx = near * (xi % 2) - near * (xi // 2)
-        dy = (yi % 2) - (yi // 2)
+        dy = near_y * (yi % 2) - near_y * (yi // 2)
         return tuple(lax.rem(at + d + size, size) for at, d, size in zip(me, (dx, dy, shift_z[zi]), sizes))
 
-    order = ((0, 0), (1, 0), (0, 1), (0, 2), (1, 1), (1, 2), (2, 1), (2, 2), (2, 0))
+    order = ((0, 0), (1, 0), (0, 1), (1, 1), (0, 2), (1, 2), (2, 1), (2, 2), (2, 0))
     peers = [(xi, yi, zi) for xi, yi in reversed(order) for zi in range(3) if (xi, yi, zi) != (0, 0, 0)]
 
     barrier = pltpu.get_barrier_semaphore()
@@ -177,7 +179,7 @@
 
         def send():
             for xi, yi, zi in peers:
-                column = order.index((xi, (3 - yi) % 3))
+                column = order.index((xi, yi))
                 rows = pl.ds(0, 8 if sub == 0 else 6)
                 source = bins.at[sub, 0, pl.ds((1, 2, 1)[zi], 2 if zi == 0 else 1), rows]
                 target = bins.at[sub, column, pl.ds((1, 0, 3)[zi], 2 if zi == 0 else 1), rows]
@@ -206,7 +208,7 @@
         def column_sums(column, slots, sums):
             xi, yi = order[column]
             offset_x = (near * (xi % 2) - near * (xi // 2)).astype(jnp.float32) - 0.5 if xi else -0.5
-            offset_y = float((yi % 2) - (yi // 2)) - 0.5
+            offset_y = (near_y * (yi % 2) - near_y * (yi // 2)).astype(jnp.float32) - 0.5 if yi else -0.5
             sums = list(sums)
             for z in slots:
                 packed = bins[sub, column, z]

time: 46.6 us -> 46.9 us (level)
  no operation moved by 1% of the time
where the time goes in v5:
time: 46.9 us; the launch traced here: 46.8 us
  Pallas kernels  45.5 us (97%)
  between operations  0.64 us (1%)
  local copies, waits for them, and re-layouts  0.6 us (1%)
    pallas_call x1, Pallas kernels, on_device(): pl.pallas_call(functools.partial(step_kernel, sizes), out_shape=pltpu.VME...  45.5 us

profile of v5, /device:TPU:1, one launch (start us, length us, event | category | flops | bytes accessed | tf_op | source)
XLA Modules:
  0.0 46.8 jit_solution(16942667781403372580)
XLA Ops:
  0.6 45.5 %shard_map.59 = f32[6,1,1,2,256]{4,3,2,1,0:T(2,128)S(1)} custom-call(f32[3,1,1,2,256]{4,3,2,1,0:T(2,128)} %positions.1, f32[3,1,1,2,256]{4,3,2,1,0:T(2,128)} %velocities.1, f32[1,1,2,256]{3,2,1,0:T(2,128)} %mass.1, s32[1,1,2]{2,1,0:T(1,128)} %counts.1), custom_call_target="tpu_custom_call" | custom-call | tf_op jit(solution)/shard_map/pallas_call | solution.py:284
  46.2 0.6 %fusion = (f32[3,1,1,2,256]{4,3,2,1,0:T(2,128)}, f32[3,1,1,2,256]{4,3,2,1,0:T(2,128)}) fusion(f32[6,1,1,2,256]{4,3,2,1,0:T(2,128)S(1)} %shard_map.59), kind=kLoop, calls=%fused_computation | loop fusion | bytes 24576 | tf_op jit(solution)/shard_map/slice | solution.py:303
